TPU v7x, 512 devices: a whole 4x8x8 slice. The times are simulated.
512 devices in a mesh: seq: 32 (over y, x), head: 16 (over z, core).
Axes of the slice: x: 4, y: 8, z: 8, core: 2. Of those that a mesh axis runs over, the one named last changes fastest.
Arguments:
- queries: bfloat16 [65536, 2048], P('seq', 'head'), may hold values from -4.5 to 4.5
- key_vectors: bfloat16 [65536, 2048], P('seq', 'head'), may hold values from -4.5 to 4.5
- value_vectors: bfloat16 [65536, 2048], P('seq', 'head'), may hold values from -18 to 18
- w_out: bfloat16 [2048, 2048], P('seq'), may hold values from -0.125 to 0.125
Outputs:
- projected: bfloat16 [65536, 2048], P(('seq', 'head'))
All inputs are finite; a program needn't handle non-finite values.
Results may differ from a plain program's by a relative error of at most 0.0053.
Values may be sent and summed in bfloat16 or wider, within the bound.
No kernel may reach another device: no remote copies, remote signals or barrier semaphores. Data moves between devices by JAX's collectives and lax.ppermute only.
A program may use at most 64 MiB of HBM per device.

v0:
```python
import math
import jax
import jax.numpy as jnp
from jax import lax
from jax.sharding import PartitionSpec as P

HD = 128
W = 1024
norm_eps = 1e-06


def passed_along(shard, axis, by):
    count = lax.axis_size(axis)
    pairs = [(i, i + by) for i in range(count) if 0 <= i + by < count]
    return lax.ppermute(shard, axis, pairs)


def carried_in(part, axis, combine, identity):
    place = lax.axis_index(axis)
    gathered = lax.all_gather(part, axis)
    state = jnp.zeros_like(part) + jnp.asarray(identity, part.dtype)

    def one(lap, state):
        return combine(state, lax.dynamic_index_in_dim(gathered, lap, 0, False))

    return lax.fori_loop(0, place, one, state)


def normalize(branch):
    return branch * lax.rsqrt(jnp.mean(branch * branch, axis=-1, keepdims=True) + norm_eps)


def add_states(earlier, later):
    return earlier + later


def split_pair(values):
    upper = lax.optimization_barrier(values.astype(jnp.bfloat16))
    lower = (values - upper.astype(jnp.float32)).astype(jnp.bfloat16)
    return (upper, lower)


def window_branch(query_heads, window_keys, window_values, offset):
    tok_rows, heads_here, head_width = query_heads.shape
    block_rows = min(512, tok_rows)
    key_span = block_rows + W
    score_scale = 1.0 / math.sqrt(head_width)

    def one_block(block_start):
        query_block = lax.dynamic_slice_in_dim(query_heads, block_start, block_rows, 0)
        key_block = lax.dynamic_slice_in_dim(window_keys, block_start, key_span, 0)
        value_block = lax.dynamic_slice_in_dim(window_values, block_start, key_span, 0)
        scores = (
            jnp.einsum("qhd,khd->hqk", query_block, key_block, preferred_element_type=jnp.float32)
            * score_scale
        )
        row_index = block_start + jnp.arange(block_rows, dtype=jnp.int32)[:, None]
        col_index = block_start + jnp.arange(key_span, dtype=jnp.int32)[None, :]
        allowed = (
            (col_index > row_index) & (col_index <= row_index + W) & (col_index - W + offset >= 0)
        )
        scores = jnp.where(allowed[None], scores, -jnp.inf)
        row_top = jnp.max(scores, axis=-1, keepdims=True)
        weights = jnp.where(allowed[None], jnp.exp(scores - row_top), 0.0).astype(jnp.bfloat16)
        return jnp.einsum("hqk,khd->qhd", weights, value_block, preferred_element_type=jnp.float32)

    starts = jnp.arange(tok_rows // block_rows, dtype=jnp.int32) * block_rows
    return lax.map(one_block, starts).reshape(tok_rows, heads_here, head_width)


def on_device(queries, key_vectors, value_vectors, w_out):
    tok_rows = queries.shape[0]
    heads_here = queries.shape[1] // HD
    head_shape = (tok_rows, heads_here, HD)
    query_heads = queries.reshape(head_shape)
    key_heads = key_vectors.reshape(head_shape)
    value_heads = value_vectors.reshape(head_shape)
    window_rim = jnp.stack([key_heads[tok_rows - W :], value_heads[tok_rows - W :]])
    earlier = passed_along(window_rim, "seq", 1)
    window_keys = jnp.concatenate([earlier[0], key_heads], axis=0)
    window_values = jnp.concatenate([earlier[1], value_heads], axis=0)
    offset = lax.axis_index("seq") * tok_rows
    soft_heads = window_branch(query_heads, window_keys, window_values, offset)
    block_rows = min(512, tok_rows)
    block_count = tok_rows // block_rows
    block_shape = (block_count, block_rows, heads_here, HD)
    blocked_queries = query_heads.reshape(block_shape)
    blocked_keys = key_heads.reshape(block_shape)
    blocked_values = value_heads.reshape(block_shape)
    state_increments = jnp.einsum(
        "bkhd,bkhe->bhde", blocked_keys, blocked_values, preferred_element_type=jnp.float32
    )
    own_total = jnp.sum(state_increments, axis=0)
    prior_state = carried_in(own_total, "seq", add_states, jnp.zeros_like(own_total))
    running = jnp.cumsum(state_increments, axis=0)
    preceding_state = prior_state[None] + jnp.concatenate(
        [jnp.zeros_like(state_increments[:1]), running[:-1]], axis=0
    )
    intra_block_scores = jnp.einsum(
        "bqhd,bkhd->bhqk", blocked_queries, blocked_keys, preferred_element_type=jnp.float32
    )
    causal = (
        jnp.arange(block_rows, dtype=jnp.int32)[:, None]
        >= jnp.arange(block_rows, dtype=jnp.int32)[None, :]
    )
    intra_block_scores = jnp.where(causal, intra_block_scores, 0.0)
    score_upper, score_lower = split_pair(intra_block_scores)
    local_block_terms = jnp.einsum(
        "bhqk,bkhd->bqhd", score_upper, blocked_values, preferred_element_type=jnp.float32
    )
    local_block_terms = local_block_terms + jnp.einsum(
        "bhqk,bkhd->bqhd", score_lower, blocked_values, preferred_element_type=jnp.float32
    )
    state_upper, state_lower = split_pair(preceding_state)
    carried_state_sum = jnp.einsum(
        "bqhd,bhde->bqhe", blocked_queries, state_upper, preferred_element_type=jnp.float32
    )
    carried_state_sum = carried_state_sum + jnp.einsum(
        "bqhd,bhde->bqhe", blocked_queries, state_lower, preferred_element_type=jnp.float32
    )
    linear = (local_block_terms + carried_state_sum).reshape(head_shape)
    mixed_heads = (0.5 * (normalize(soft_heads) + normalize(linear))).astype(jnp.bfloat16)
    mixed_heads = mixed_heads.reshape(tok_rows, heads_here * HD)
    regrouped = lax.all_to_all(mixed_heads, "head", split_axis=0, concat_axis=1, tiled=True)
    projected = jnp.dot(
        regrouped,
        lax.all_gather(w_out, "seq", axis=0, tiled=True),
        preferred_element_type=jnp.float32,
    )
    return projected.astype(jnp.bfloat16)


def solution(mesh):
    placed = (P("seq", "head"), P("seq", "head"), P("seq", "head"), P("seq", None))
    return jax.shard_map(
        on_device, mesh=mesh, in_specs=placed, out_specs=P(("seq", "head"), None), check_vma=False
    )
```

profile of v0, /device:TPU:1, one launch (start us, length us, event | category | flops | bytes accessed | tf_op | source)
XLA Modules:
  0.0 214.6 jit_solution(4155699273040618494)
XLA Ops:
  6.5 2.3 %fusion.41 = (f32[128,128]{1,0:T(8,128)}, f32[4,128,128]{2,1,0:T(8,128)S(1)}) fusion(bf16[4,512,128]{2,1,0:T(8,128)(2,1)} %bitcast.109, bf16[4,512,128]{2,1,0:T(8,128)(2,1)} %bitcast.105), kind=kOutput, calls=%fused_computation.63 | convolution fusion | flops 67158016 | bytes 1376256 | tf_op jit(solution)/shard_map/bkhd,bkhe->bhde/dot_general | solution.py:90
  9.6 1.1 slice_bitcast_fusion.2
  10.6 0.8 pad_maximum_fusion.2
  11.5 4.7 %collective-permute-start = (bf16[2,1024,1,128]{3,1,2,0:T(8,128)(2,1)}, bf16[2,1024,1,128]{3,1,2,0:T(8,128)(2,1)}, u32[]{:S(2)}, u32[]{:S(2)}) collective-permute-start(bf16[2,1024,1,128]{3,1,2,0:T(8,128)(2,1)} %pad_maximum_fusion.2), channel_id=1, source_target_pairs={{0,16},{16,32},{32,48},{48,64},{64,80},{80,96},{96,112},{112,128},... | collective-permute-start | bytes 1572872 | tf_op jit(solution)/shard_map/ppermute | solution.py:15
  18.1 1.8 fusion.16
  20.6 0.9 slice.24
  21.6 2.9 %fusion.26 = f32[4,128,512]{1,2,0:T(8,128)} fusion(f32[4,512,128]{2,1,0:T(8,128)} %fusion.16, bf16[4,512,128]{2,1,0:T(8,128)(2,1)S(1)} %bitcast.107, bf16[4,1,512,512]{3,2,0,1:T(8,128)(2,1)S(1)} %fusion.14), kind=kOutput, calls=%fused_computation.35 | convolution fusion | flops 268697600 | bytes 4718592 | tf_op jit(solution)/shard_map/bhqk,bkhd->bqhd/dot_general | solution.py:108
  24.5 1.1 slice_bitcast_fusion
  25.8 36.6 %while.22 = (s32[]{:T(128)}, f32[4,512,1,128]{1,3,2,0:T(8,128)}, s32[4]{0:T(128)S(1)}, bf16[3072,1,128]{2,0,1:T(8,128)(2,1)S(1)}, s32[]{:T(128)}, /*index=5*/bf1...) while((s32[]{:T(128)}, f32[4,512,1,128]{1,3,2,0:T(8,128)}, ...), condition=%wide.region_2.3_spmd, body=%wide.region_0.2_spmd.sunk | while | flops 413671424 | bytes 7516368 | solution.py:68
  31.6 1.2 fusion.57
  32.8 2.1 fusion.58
  40.7 1.2 fusion.57
  41.9 2.1 fusion.58
  49.9 1.2 fusion.57
  51.1 2.2 %fusion.58 = f32[4,512,1,128]{1,3,2,0:T(8,128)} fusion(f32[4,512,1,128]{1,3,2,0:T(8,128)} %get-tuple-element.263, s32[]{:T(128)} %get-tuple-element.262, f32[512,1536]{1,0:T(8,128)S(1)} %get-tuple-element.224, f32[512]{0:T(512)S(1)} %get-tuple-element.225, s32[1536]{0:T(1024)S(1)} %iota_add_fusion.5, s32[512]{0:T(512)S(1)} %get-tuple-element.222, ...), kind=kOutput, calls=%fused_computation.6.clone.1 | convolution fusion | flops 206831616 | bytes 3817988 | tf_op jit(solution)/shard_map/while/body/eval_jaxpr/hqk,khd->qhd/dot_general | solution.py:65
  59.0 1.2 fusion.57
  60.2 2.2 %fusion.58 = f32[4,512,1,128]{1,3,2,0:T(8,128)} fusion(f32[4,512,1,128]{1,3,2,0:T(8,128)} %get-tuple-element.263, s32[]{:T(128)} %get-tuple-element.262, f32[512,1536]{1,0:T(8,128)S(1)} %get-tuple-element.224, f32[512]{0:T(512)S(1)} %get-tuple-element.225, s32[1536]{0:T(1024)S(1)} %iota_add_fusion.5, s32[512]{0:T(512)S(1)} %get-tuple-element.222, ...), kind=kOutput, calls=%fused_computation.6.clone.1 | convolution fusion | flops 206831616 | bytes 3817988 | tf_op jit(solution)/shard_map/while/body/eval_jaxpr/hqk,khd->qhd/dot_general | solution.py:65
  62.4 1.5 copy.11
  63.9 1.4 multiply_reduce_fusion
  65.3 29.2 %all-gather.6.cloned.1.call-done = f32[4096,128]{1,0:T(8,128)} async-done(((f32[128,128]{1,0:T(8,128)}), f32[4096,128]{1,0:T(8,128)}) %all-gather.6.cloned.1.call-update) | async-done | bytes 2097168 | tf_op jit(solution)/shard_map/all_gather | solution.py:20
  94.8 1.7 fusion.29
  97.3 29.8 %all_to_all.16 = bf16[16,128,128]{2,1,0:T(8,128)(2,1)S(1)} all-to-all(bf16[16,128,128]{2,1,0:T(8,128)(2,1)S(1)} %multiply_convert_fusion), channel_id=1, replica_groups=mesh['seq'=32,'head'=16] {'head'}, dimensions={0} | all-to-all | bytes 1048576 | tf_op jit(solution)/shard_map/all_to_all | solution.py:124
  127.4 74.9 %all-gather.4.cloned.1.call-done = bf16[2048,2048]{1,0:T(8,128)(2,1)} async-done(((bf16[64,2048]{1,0:T(8,128)(2,1)}), bf16[2048,2048]{1,0:T(8,128)(2,1)}) %all-gather.4.cloned.1.call-update) | async-done | bytes 8388624 | tf_op jit(solution)/shard_map/all_gather | solution.py:127
  202.3 5.5 %convolution_convert_fusion = bf16[128,2048]{1,0:T(8,128)(2,1)} fusion(bf16[128,2048]{0,1:T(8,128)(2,1)S(1)} %bitcast.116, bf16[2048,2048]{1,0:T(8,128)(2,1)} %all-gather.4.cloned.1.call-done), kind=kOutput, calls=%fused_computation.24 | convolution fusion | flops 1074003968 | bytes 9437184 | tf_op jit(solution)/shard_map/dot_general | solution.py:125
  (47 shorter events, 14.9 us)
Async XLA Ops:
  6.5 9.8 %copy-start.1 = (bf16[2048,128]{1,0:T(8,128)(2,1)S(1)}, bf16[2048,128]{1,0:T(8,128)(2,1)}, u32[]{:S(2)}) copy-start(bf16[2048,128]{1,0:T(8,128)(2,1)} %param.9) | copy-start | bytes 1572868
  6.5 9.8 %copy-start.2 = (bf16[2048,128]{1,0:T(8,128)(2,1)S(1)}, bf16[2048,128]{1,0:T(8,128)(2,1)}, u32[]{:S(2)}) copy-start(bf16[2048,128]{1,0:T(8,128)(2,1)} %param.8) | copy-start | bytes 1572868
  6.5 88.0 %all-gather.6.cloned.1.call-start = ((), (), s32[]{:S(2)}) async-start(), calls=%async_computation.2 | async-start | bytes 2162688 | tf_op jit(solution)/shard_map/all_gather | solution.py:20
  8.8 193.5 %all-gather.4.cloned.1.call-start = ((), (), s32[]{:S(2)}) async-start(), calls=%async_computation.1 | async-start | bytes 8650752 | tf_op jit(solution)/shard_map/all_gather | solution.py:127
  11.5 13.0 %collective-permute-start = (bf16[2,1024,1,128]{3,1,2,0:T(8,128)(2,1)}, bf16[2,1024,1,128]{3,1,2,0:T(8,128)(2,1)}, u32[]{:S(2)}, u32[]{:S(2)}) collective-permute-start(bf16[2,1024,1,128]{3,1,2,0:T(8,128)(2,1)} %pad_maximum_fusion.2), channel_id=1, source_target_pairs={{0,16},{16,32},{32,48},{48,64},{64,80},{80,96},{96,112},{112,128},... | collective-permute-start | bytes 1572872 | tf_op jit(solution)/shard_map/ppermute | solution.py:15
  17.0 1.0 copy-start
  24.5 1.3 copy-start.3
Sparse Core Ops, SparseCore 0:
  10.5 83.9 all-gather.5
  97.7 104.5 all-gather.3
where the time goes:
time: 217 us; the launch traced here: 215 us
  waiting for transfers between devices  105 us (48%)
  blocking collectives  29.8 us (14%)
  matrix products  28.6 us (13%)
  between operations  13.5 us (6%)
  loops' own time  13 us (6%)
  other arithmetic  12.3 us (6%)
  local copies, waits for them, and re-layouts  7.72 us (4%)
  starting transfers between devices  4.79 us (2%)
    all_gather x1, waiting for transfers between devices, on_device(): lax.all_gather(w_out, 'seq', axis=0, tiled=True)  74.9 us
    all_to_all x1, blocking collectives, on_device(): lax.all_to_all(mixed_heads, 'head', split_axis=0, concat_axis=1, tiled=True)  29.8 us
    all_gather x1, waiting for transfers between devices, carried_in(): gathered = lax.all_gather(part, axis)  29.2 us
    another operation x1, loops' own time, window_branch(): return lax.map(one_block, starts).reshape(tok_rows, heads_here, head_width)  13 us
    dot_general x4, matrix products, one_block(): jnp.einsum('hqk,khd->qhd', weights, value_block, preferred_element_type=j...  8.59 us
    dot_general x1, matrix products, on_device(): jnp.dot(regrouped, lax.all_gather(w_out, 'seq', axis=0, tiled=True), pref...  5.45 us
    dot_general x4, matrix products, one_block(): jnp.einsum('qhd,khd->hqk', query_block, key_block, preferred_element_type...  4.85 us
    ppermute x1, starting transfers between devices, passed_along(): return lax.ppermute(shard, axis, pairs)  4.74 us
  transfers between devices with their start and end apart: 3, of which 2 were waited for; matrix products, arithmetic and copies ran while one was open for 19% of the time, Pallas kernels for 0%

commit v1 on v0

--- a/solution.py
+++ b/solution.py
@@ -124,7 +124,9 @@
     regrouped = lax.all_to_all(mixed_heads, "head", split_axis=0, concat_axis=1, tiled=True)
     projected = jnp.dot(
         regrouped,
-        lax.all_gather(w_out, "seq", axis=0, tiled=True),
+        jnp.concatenate(
+            lax.all_to_all(jnp.stack([w_out] * lax.axis_size("seq")), "seq", 0, 0), axis=0
+        ),
         preferred_element_type=jnp.float32,
     )
     return projected.astype(jnp.bfloat16)

time: 217 us -> 374 us (1.72)
  the two profiles are of different devices: /device:TPU:1 before, /device:TPU:31 now
where the time goes in v1:
time: 374 us; the launch traced here: 372 us
  waiting for transfers between devices  224 us (60%)
  blocking collectives  30.1 us (8%)
  matrix products  28.6 us (8%)
  other arithmetic  26.4 us (7%)
  starting transfers between devices  23.8 us (6%)
  between operations  13.6 us (4%)
  loops' own time  13.4 us (4%)
  local copies, waits for them, and re-layouts  12 us (3%)
    all_to_all x1, waiting for transfers between devices, on_device(): lax.all_to_all(jnp.stack([w_out] * lax.axis_size('seq')), 'seq', 0, 0)  198 us
    all_to_all x1, blocking collectives, on_device(): lax.all_to_all(mixed_heads, 'head', split_axis=0, concat_axis=1, tiled=True)  30.1 us
    all_gather x1, waiting for transfers between devices, carried_in(): gathered = lax.all_gather(part, axis)  23.3 us
    all_to_all x1, starting transfers between devices, on_device(): lax.all_to_all(jnp.stack([w_out] * lax.axis_size('seq')), 'seq', 0, 0)  19.5 us
    another operation x1, loops' own time, window_branch(): return lax.map(one_block, starts).reshape(tok_rows, heads_here, head_width)  13.1 us
    add x15, other arithmetic, add_states(): return earlier + later  12.9 us
    dot_general x4, matrix products, one_block(): jnp.einsum('hqk,khd->qhd', weights, value_block, preferred_element_type=j...  8.58 us
  transfers between devices with their start and end apart: 3, of which 3 were waited for; matrix products, arithmetic and copies ran while one was open for 10% of the time, Pallas kernels for 0%

profile of v1, /device:TPU:31, one launch (start us, length us, event | category | flops | bytes accessed | tf_op | source)
XLA Modules:
  0.0 371.6 jit_solution(486657727391249804)
XLA Ops:
  6.5 2.2 fusion.41
  10.7 4.3 %collective-permute-start = (bf16[2,1024,1,128]{3,1,2,0:T(8,128)(2,1)}, bf16[2,1024,1,128]{3,1,2,0:T(8,128)(2,1)}, u32[]{:S(2)}, u32[]{:S(2)}) collective-permute-start(bf16[2,1024,1,128]{3,1,2,0:T(8,128)(2,1)} %pad_maximum_fusion.2), channel_id=1, source_target_pairs={{0,16},{16,32},{32,48},{48,64},{64,80},{80,96},{96,112},{112,128},... | collective-permute-start | bytes 1572872 | tf_op jit(solution)/shard_map/ppermute | solution.py:15
  16.9 1.8 fusion.16
  20.4 2.9 fusion.26
  23.3 2.6 collective-permute-done
  28.0 37.0 %while.22 = (s32[]{:T(128)}, f32[4,512,1,128]{1,3,2,0:T(8,128)}, s32[4]{0:T(128)S(1)}, bf16[3072,1,128]{2,0,1:T(8,128)(2,1)}, s32[]{:T(128)}, /*index=5*/bf16[20...) while((s32[]{:T(128)}, f32[4,512,1,128]{1,3,2,0:T(8,128)}, ...), condition=%wide.region_2.3_spmd, body=%wide.region_0.2_spmd.sunk | while | flops 413671424 | bytes 10661624 | solution.py:68
  33.9 1.2 fusion.57
  35.1 2.1 fusion.58
  43.1 1.2 fusion.57
  44.4 2.1 fusion.58
  52.4 1.2 fusion.57
  53.6 2.1 fusion.58
  61.6 1.2 fusion.57
  62.8 2.2 fusion.58
  65.0 1.5 copy.11
  66.6 1.4 multiply_reduce_fusion
  67.9 23.3 %all-gather.3.cloned.1.call-done = f32[4096,128]{1,0:T(8,128)} async-done(((f32[128,128]{1,0:T(8,128)}), f32[4096,128]{1,0:T(8,128)}) %all-gather.3.cloned.1.call-update) | async-done | bytes 2097168 | tf_op jit(solution)/shard_map/all_gather | solution.py:20
  91.3 13.2 %while.23 = (s32[]{:T(128)}, f32[1,128,128]{2,1,0:T(8,128)S(1)}, s32[]{:T(128)}, f32[32,1,128,128]{3,2,1,0:T(8,128)}, s32[]{:T(128)}, /*index=5*/s32[]{:T(128)}, s32[]{:T(128)}) while((s32[]{:T(128)}, f32[1,128,128]{2,1,0:T(8,128)S(1)}, s32[]{:T(128)}, f32[32,1,128,128]{3,2,1,0:T(8,128)}, s32[]{:T(128)}, /*index=5*/s32[]{:T(128)}, ...), condition=%wide.region_6.7_spmd, body=%wide.region_5.6_spmd.sunk | while | flops 16389 | bytes 196731 | solution.py:26
  104.8 1.8 fusion.29
  107.3 30.1 %all_to_all.21 = bf16[16,128,128]{2,1,0:T(8,128)(2,1)S(1)} all-to-all(bf16[16,128,128]{2,1,0:T(8,128)(2,1)S(1)} %multiply_convert_fusion), channel_id=1, replica_groups=mesh['seq'=32,'head'=16] {'head'}, dimensions={0} | all-to-all | bytes 1048576 | tf_op jit(solution)/shard_map/all_to_all | solution.py:124
  137.5 4.3 %stack.11 = bf16[32,64,2048]{2,1,0:T(8,128)(2,1)} broadcast(bf16[64,2048]{1,0:T(8,128)(2,1)S(1)} %copy-done.5), dimensions={1,2} | broadcast | bytes 8650752 | tf_op jit(solution)/shard_map/stack | solution.py:128
  141.7 19.5 %all-to-all-start.1 = ((bf16[32,64,2048]{2,1,0:T(8,128)(2,1)}), bf16[32,64,2048]{2,1,0:T(8,128)(2,1)}, u32[]{:S(2)}, u32[]{:S(2)}) async-start(bf16[32,64,2048]{2,1,0:T(8,128)(2,1)} %stack.11), calls=%async_computation.1 | async-start | bytes 16777216 | tf_op jit(solution)/shard_map/all_to_all | solution.py:128
  161.5 197.8 %all-to-all-done.1 = bf16[32,64,2048]{2,1,0:T(8,128)(2,1)} async-done(((bf16[32,64,2048]{2,1,0:T(8,128)(2,1)}), bf16[32,64,2048]{2,1,0:T(8,128)(2,1)}, u32[]{:S(2)}, u32[]{:S(2)}) %all-to-all-start.1) | async-done | bytes 8388640 | tf_op jit(solution)/shard_map/all_to_all | solution.py:128
  359.3 5.5 %convolution_convert_fusion = bf16[128,2048]{1,0:T(8,128)(2,1)} fusion(bf16[128,2048]{0,1:T(8,128)(2,1)S(1)} %bitcast.117, bf16[2048,2048]{1,0:T(8,128)(2,1)} %bitcast.35), kind=kOutput, calls=%fused_computation.24 | convolution fusion | flops 1074003968 | bytes 9437184 | tf_op jit(solution)/shard_map/dot_general | solution.py:125
  (72 shorter events, 32.1 us)
Async XLA Ops:
  6.5 8.6 %copy-start.1 = (bf16[2048,128]{1,0:T(8,128)(2,1)S(1)}, bf16[2048,128]{1,0:T(8,128)(2,1)}, u32[]{:S(2)}) copy-start(bf16[2048,128]{1,0:T(8,128)(2,1)} %param.9) | copy-start | bytes 1572868
  6.5 8.6 %copy-start.2 = (bf16[2048,128]{1,0:T(8,128)(2,1)S(1)}, bf16[2048,128]{1,0:T(8,128)(2,1)}, u32[]{:S(2)}) copy-start(bf16[2048,128]{1,0:T(8,128)(2,1)} %param.8) | copy-start | bytes 1572868
  6.5 84.7 %all-gather.3.cloned.1.call-start = ((), (), s32[]{:S(2)}) async-start(), calls=%async_computation.2 | async-start | bytes 2162688 | tf_op jit(solution)/shard_map/all_gather | solution.py:20
  10.7 15.2 %collective-permute-start = (bf16[2,1024,1,128]{3,1,2,0:T(8,128)(2,1)}, bf16[2,1024,1,128]{3,1,2,0:T(8,128)(2,1)}, u32[]{:S(2)}, u32[]{:S(2)}) collective-permute-start(bf16[2,1024,1,128]{3,1,2,0:T(8,128)(2,1)} %pad_maximum_fusion.2), channel_id=1, source_target_pairs={{0,16},{16,32},{32,48},{48,64},{64,80},{80,96},{96,112},{112,128},... | collective-permute-start | bytes 1572872 | tf_op jit(solution)/shard_map/ppermute | solution.py:15
  15.9 1.0 copy-start
  23.3 4.7 %copy-start.3 = (bf16[2048,128]{1,0:T(8,128)(2,1)S(1)}, bf16[2048,128]{1,0:T(8,128)(2,1)}, u32[]{:S(2)}) copy-start(bf16[2048,128]{1,0:T(8,128)(2,1)} %param.8) | copy-start | bytes 1572868
  32.5 2.6 copy-start.4
  41.7 2.6 copy-start.4
  51.0 2.6 copy-start.4
  60.2 2.6 copy-start.4
  104.8 32.7 %copy-start.5 = (bf16[64,2048]{1,0:T(8,128)(2,1)S(1)}, bf16[64,2048]{1,0:T(8,128)(2,1)}, u32[]{:S(2)}) copy-start(bf16[64,2048]{1,0:T(8,128)(2,1)} %param.11) | copy-start | bytes 786436
  141.7 217.6 %all-to-all-start.1 = ((bf16[32,64,2048]{2,1,0:T(8,128)(2,1)}), bf16[32,64,2048]{2,1,0:T(8,128)(2,1)}, u32[]{:S(2)}, u32[]{:S(2)}) async-start(bf16[32,64,2048]{2,1,0:T(8,128)(2,1)} %stack.11), calls=%async_computation.1 | async-start | bytes 16777216 | tf_op jit(solution)/shard_map/all_to_all | solution.py:128
Sparse Core Ops, SparseCore 0:
  10.5 80.7 all-gather.2
